TPU v7x, 512 devices: a whole 4x8x8 slice. The times are simulated.
512 devices in a mesh: row: 16 (over z, core), col: 32 (over x, y).
Axes of the slice: x: 4, y: 8, z: 8, core: 2. Of those that a mesh axis runs over, the one named last changes fastest.
Arguments:
- strip: float32 [20480, 128], P('row'), may hold values from -6 to 6
- block_below: float32 [64, 64], replicated, may hold values from -1 to 1
- inverse_first: float32 [64, 64], replicated, may hold values from -0.5 to 1.5, as said below
- inverse_second: float32 [64, 64], replicated, may hold values from -0.5 to 1.5, as said below
- cotangent: float32 [20480, 20480], P('row', 'col'), may hold values from -0.0390625 to 0.0390625
Outputs:
- strip_grad: float32 [20480, 128], P('row')
Inputs may be any that keep to these rules, and one draw needn't show every extreme that they name: inverse_first is lower triangular with its diagonal in 0.5 to 1.5. inverse_second is lower triangular with its diagonal in 0.5 to 1.5.
All inputs are finite; a program needn't handle non-finite values.
Results may differ from a plain program's by a relative error of at most 0.00007.
Values sent between devices are 32-bit elements; how exact they have to be, the bound alone decides.
A program may use at most 64 MiB of HBM per device.

v0:
```python
import jax
import jax.numpy as jnp
from jax import lax
from jax.sharding import PartitionSpec as P


def from_root(value, axis, source):
    kept = jnp.where(lax.axis_index(axis) == source, value, 0).astype(value.dtype)
    return lax.psum(kept, axis)


def mul(left, right):
    return jnp.dot(left, right, precision=lax.Precision.HIGHEST, preferred_element_type=jnp.float32)


def finish(bar_sum, left_block, inverse_first, inverse_second, panel):
    bar_updated = mul(-bar_sum[:, panel:], inverse_second)
    bar_first = -bar_sum[:, :panel] - mul(bar_updated, left_block)
    return jnp.concatenate([mul(bar_first, inverse_first), bar_updated], axis=1)


def shards(strip, block_below, inverse_first, inverse_second, cotangent):
    panel = inverse_first.shape[0]
    cols_here = cotangent.shape[1]
    ratio = lax.axis_size("col") // lax.axis_size("row")
    col_id = lax.axis_index("col")
    owner = col_id // ratio
    offset = col_id % ratio * cols_here
    lower_first = mul(strip[:, :panel], inverse_first.T)
    left_block = mul(block_below, inverse_first.T)
    updated = strip[:, panel:] - mul(lower_first, left_block.T)
    col_first = from_root(lax.dynamic_slice_in_dim(lower_first, offset, cols_here, 0), "row", owner)
    lower_second = mul(updated, inverse_second.T)
    col_second = from_root(
        lax.dynamic_slice_in_dim(lower_second, offset, cols_here, 0), "row", owner
    )
    col_lower = jnp.concatenate([col_first, col_second], axis=1)
    lower = jnp.concatenate([lower_first, lower_second], axis=1)
    transposed = lax.dot_general(
        cotangent,
        lower,
        (((0,), (0,)), ((), ())),
        precision=lax.Precision.HIGHEST,
        preferred_element_type=jnp.float32,
    )
    col_total = lax.psum(transposed, "row")
    row_index = lax.axis_index("row")
    pieces = []
    for member in range(ratio):
        pieces.append(from_root(col_total, "col", row_index * ratio + member))
    routed = jnp.concatenate(pieces, axis=0)
    local_sum = mul(cotangent, col_lower)
    row_total = lax.psum(local_sum, "col")
    row_total = row_total + routed
    return finish(row_total, left_block, inverse_first, inverse_second, panel)


def solution(mesh):
    return jax.shard_map(
        shards,
        mesh=mesh,
        in_specs=(P("row", None), P(), P(), P(), P("row", "col")),
        out_specs=P("row", None),
        check_vma=False,
    )
```

profile of v0, /device:TPU:64, one launch (start us, length us, event | category | flops | bytes accessed | tf_op | source)
XLA Modules:
  0.0 320.7 jit_solution(9730919756724847951)
XLA Ops:
  6.5 0.0 copy-start
  6.5 0.0 all-reduce.7.cloned.1.call-start
  6.5 1.1 fusion.11
  7.7 2.7 fusion.3
  10.3 0.0 copy-start.1
  10.3 2.5 convolution_subtract_fusion
  12.8 1.6 fusion.12
  14.5 0.0 copy-done
  14.5 3.8 %convolution_bitcast_fusion.1 = f32[640,128]{0,1:T(8,128)} fusion(f32[1280,640]{1,0:T(8,128)S(1)} %copy-done, f32[1280,64]{0,1:T(8,128)S(1)} %fusion.12, f32[1280,64]{0,1:T(8,128)} %fusion.3), kind=kOutput, calls=%fused_computation.3 | convolution fusion | flops 1258455040 | bytes 4259840 | tf_op jit(solution)/shard_map/dot_general | solution.py:39
  18.3 0.0 copy-done.1
  18.3 0.7 dynamic-slice_select_fusion
  19.1 0.0 all-reduce.7.cloned.1.call-update
  19.1 0.0 all-reduce.5.cloned.1.call-start
  19.1 118.0 %all-reduce.7.cloned.1.call-done = (f32[640,64]{0,1:T(8,128)}, f32[640,64]{0,1:T(8,128)}, f32[640,128]{0,1:T(8,128)}) async-done(((f32[640,64]{0,1:T(8,128)}, f32[640,64]{0,1:T(8,128)}, f32[640,128]{0,1:T(8,128)}), (f32[640,64]{0,1:T(8,128)}, f32[640,64]{0,1:T(8,128)}, f32[640,128]{0,1:T(8,128)})) %all-reduce.7.cloned.1.call-update) | async-done | bytes 655376 | tf_op jit(solution)/shard_map/psum | solution.py:9
  137.2 0.0 copy-start.2
  137.2 0.0 copy-start.4
  137.2 5.3 %convolution_bitcast_fusion = f32[1280,128]{0,1:T(8,128)} fusion(f32[1280,640]{1,0:T(8,128)S(1)} %copy-done, f32[640,64]{0,1:T(8,128)} %get-tuple-element.8, f32[640,64]{0,1:T(8,128)} %get-tuple-element.9), kind=kOutput, calls=%fused_computation.1 | convolution fusion | flops 1258373120 | bytes 4259840 | tf_op jit(solution)/shard_map/dot_general | solution.py:13
  142.5 0.0 copy-start.3
  142.5 0.0 copy-done.2
  142.5 0.9 broadcast_select_fusion.1
  143.4 0.0 all-reduce.5.cloned.1.call-update
  143.4 164.6 %all-reduce.5.cloned.1.call-done = (f32[1280,128]{0,1:T(8,128)}, f32[640,128]{0,1:T(8,128)}, f32[640,128]{0,1:T(8,128)}) async-done(((f32[1280,128]{0,1:T(8,128)}, f32[640,128]{0,1:T(8,128)}, f32[640,128]{0,1:T(8,128)}), (f32[1280,128]{0,1:T(8,128)}, f32[640,128]{0,1:T(8,128)}, f32[640,128]{0,1:T(8,128)})) %all-reduce.5.cloned.1.call-update) | async-done | bytes 1310736 | tf_op jit(solution)/shard_map/psum | solution.py:53
  308.0 1.3 maximum_add_fusion
  309.3 0.0 copy-done.4
  309.4 0.5 fusion.5
  309.8 0.5 convolution_subtract_fusion.1
  310.3 0.0 copy-done.3
  310.3 0.5 fusion.13
  310.8 0.9 pad_maximum_fusion
  311.7 2.2 copy.6
Async XLA Ops:
  6.5 7.9 %copy-start = (f32[1280,640]{1,0:T(8,128)S(1)}, f32[1280,640]{1,0:T(8,128)}, u32[]{:S(2)}) copy-start(f32[1280,640]{1,0:T(8,128)} %param.9) | copy-start | bytes 9830404
  6.5 130.6 %all-reduce.7.cloned.1.call-start = ((), (), s32[]{:S(2)}) async-start(), calls=%async_computation.1 | async-start | bytes 1310720 | tf_op jit(solution)/shard_map/psum | solution.py:9
  10.3 8.0 %copy-start.1 = (f32[1280,64]{0,1:T(8,128)S(1)}, f32[1280,64]{0,1:T(8,128)}, u32[]{:S(2)}) copy-start(f32[1280,64]{0,1:T(8,128)} %fusion.3) | copy-start | bytes 983044
  19.1 288.9 %all-reduce.5.cloned.1.call-start = ((), (), s32[]{:S(2)}) async-start(), calls=%async_computation | async-start | bytes 2621440 | tf_op jit(solution)/shard_map/psum | solution.py:53
  137.2 5.3 %copy-start.2 = (f32[640,128]{0,1:T(8,128)S(1)}, f32[640,128]{0,1:T(8,128)}, u32[]{:S(2)}) copy-start(f32[640,128]{0,1:T(8,128)} %get-tuple-element.10) | copy-start | bytes 983044
  137.2 172.2 %copy-start.4 = (f32[64,64]{1,0:T(8,128)S(1)}, f32[64,64]{1,0:T(8,128)}, u32[]{:S(2)}) copy-start(f32[64,64]{1,0:T(8,128)} %param.8) | copy-start | bytes 49156
  142.5 167.8 %copy-start.3 = (f32[64,64]{1,0:T(8,128)S(1)}, f32[64,64]{1,0:T(8,128)}, u32[]{:S(2)}) copy-start(f32[64,64]{1,0:T(8,128)} %param.7) | copy-start | bytes 49156
Sparse Core Ops, SparseCore 0:
  19.2 117.9 all-reduce.6
  143.5 164.4 all-reduce.4
where the time goes:
time: 321 us
  waiting for transfers between devices  283 us (88%)
  matrix products  18.5 us (6%)
  between operations  13.5 us (4%)
  other arithmetic  3.85 us (1%)
    psum x1, waiting for transfers between devices, shards(): row_total = lax.psum(local_sum, 'col')  165 us
    psum x1, waiting for transfers between devices, from_root(): return lax.psum(kept, axis)  118 us
    dot_general x8, matrix products, mul(): jnp.dot(left, right, precision=lax.Precision.HIGHEST, preferred_element_t...  14.6 us
  transfers between devices with their start and end apart: 2, of which 2 were waited for; matrix products, arithmetic and copies ran while one was open for 0% of the time, Pallas kernels for 0%

commit v1 on v0

--- a/solution.py
+++ b/solution.py
@@ -6,7 +6,7 @@
 
 def from_root(value, axis, source):
     kept = jnp.where(lax.axis_index(axis) == source, value, 0).astype(value.dtype)
-    return lax.psum(kept, axis)
+    return jnp.sum(lax.all_gather(kept, axis), axis=0)
 
 
 def mul(left, right):

time: 321 us -> 629 us (1.96)
  waiting for transfers between devices: 283 us -> 551 us
  local copies, waits for them, and re-layouts: 2.18 us -> 28.5 us
  other arithmetic: 3.85 us -> 19.5 us
    all_gather x0 -> x4, waiting for transfers between devices: none -> 299 us  [from_root(): return jnp.sum(lax.all_gather(kept, axis), axis=0)]
    unnamed x10 -> x16, local copies, waits for them, and re-layouts: 0.02 us -> 26.3 us
    psum x1, waiting for transfers between devices: 165 us -> 139 us  [shards(): row_total = lax.psum(local_sum, 'col')]
    reduce_sum x0 -> x2, other arithmetic: none -> 12.2 us  [from_root(): return jnp.sum(lax.all_gather(kept, axis), axis=0)]
  transfers between devices with their start and end apart: 2 -> 6, of which waited for: 2 -> 6; matrix products, arithmetic and copies ran while one was open for 0% -> 7% of each run, Pallas kernels for 0% -> 0%
where the time goes in v1:
time: 629 us
  waiting for transfers between devices  551 us (88%)
  local copies, waits for them, and re-layouts  28.5 us (5%)
  other arithmetic  19.5 us (3%)
  matrix products  15.7 us (2%)
  between operations  13.6 us (2%)
    all_gather x4, waiting for transfers between devices, from_root(): return jnp.sum(lax.all_gather(kept, axis), axis=0)  299 us
    psum x1, waiting for transfers between devices, shards(): row_total = lax.psum(local_sum, 'col')  139 us
    psum x1, waiting for transfers between devices, shards(): col_total = lax.psum(transposed, 'row')  112 us
    unnamed x16, local copies, waits for them, and re-layouts  26.3 us
    dot_general x8, matrix products, mul(): jnp.dot(left, right, precision=lax.Precision.HIGHEST, preferred_element_t...  12.8 us
  transfers between devices with their start and end apart: 6, of which 6 were waited for; matrix products, arithmetic and copies ran while one was open for 7% of the time, Pallas kernels for 0%

profile of v1, /device:TPU:64, one launch (start us, length us, event | category | flops | bytes accessed | tf_op | source)
XLA Modules:
  0.0 628.7 jit_solution(7800177671469841524)
XLA Ops:
  6.5 0.0 copy-start
  6.5 0.0 all-reduce.5.cloned.1.call-start
  6.5 1.1 fusion.11
  7.7 1.9 fusion.3
  9.6 0.0 copy-start.2
  9.6 2.5 convolution_subtract_fusion
  12.1 1.6 fusion.12
  13.7 0.0 copy-done.2
  13.7 0.0 copy-start.3
  13.7 0.7 copy-done.3
  14.4 0.0 copy-done
  14.4 2.9 convolution_bitcast_fusion.1
  17.3 0.0 all-reduce.5.cloned.1.call-update
  17.3 0.0 all-gather.9.cloned.1.call-start
  17.4 1.6 dynamic-slice_select_fusion.1
  19.0 0.0 all-gather.9.cloned.1.call-update
  19.0 0.0 all-gather.11.cloned.1.call-start
  19.1 1.6 dynamic-slice_select_fusion
  20.7 0.0 all-gather.11.cloned.1.call-update
  20.7 0.0 all-gather.13.cloned.1.call-start
  20.8 112.1 %all-reduce.5.cloned.1.call-done = f32[640,128]{0,1:T(8,128)} async-done(((f32[640,128]{0,1:T(8,128)}), f32[640,128]{0,1:T(8,128)}) %all-reduce.5.cloned.1.call-update) | async-done | bytes 327696 | tf_op jit(solution)/shard_map/psum | solution.py:46
  132.8 1.9 broadcast_select_fusion.1
  134.7 0.0 all-gather.13.cloned.1.call-update
  134.7 0.0 all-gather.15.cloned.1.call-start
  134.8 0.5 all-gather.15.cloned.1.call-update
  135.3 0.2 all-reduce.3.cloned.1.call-start
  135.5 43.4 %all-gather.9.cloned.1.call-done = f32[10240,64]{0,1:T(8,128)} async-done(((f32[640,64]{0,1:T(8,128)}), f32[10240,64]{0,1:T(8,128)}) %all-gather.9.cloned.1.call-update) | async-done | bytes 2621456 | tf_op jit(solution)/shard_map/all_gather | solution.py:9
  179.0 3.7 copy.8
  182.7 40.6 %all-gather.11.cloned.1.call-done = f32[10240,64]{0,1:T(8,128)} async-done(((f32[640,64]{0,1:T(8,128)}), f32[10240,64]{0,1:T(8,128)}) %all-gather.11.cloned.1.call-update) | async-done | bytes 2621456 | tf_op jit(solution)/shard_map/all_gather | solution.py:9
  223.3 2.4 copy.9
  225.6 0.2 copy-done.1
  225.8 0.9 bitcast_reduce_fusion.2
  226.7 4.3 convolution_bitcast_fusion
  231.0 0.0 all-reduce.3.cloned.1.call-update
  231.0 109.2 %all-gather.13.cloned.1.call-done = f32[20480,128]{0,1:T(8,128)} async-done(((f32[640,128]{0,1:T(8,128)}), f32[20480,128]{0,1:T(8,128)}) %all-gather.13.cloned.1.call-update) | async-done | bytes 10485776 | tf_op jit(solution)/shard_map/all_gather | solution.py:9
  340.2 9.7 %copy.10 = f32[16,8,32,640]{3,2,1,0:T(8,128)} copy(f32[16,8,32,640]{3,1,2,0:T(8,128)} %bitcast.38) | data formatting | bytes 20971520
  349.9 105.7 %all-gather.15.cloned.1.call-done = f32[20480,128]{0,1:T(8,128)} async-done(((f32[640,128]{0,1:T(8,128)}), f32[20480,128]{0,1:T(8,128)}) %all-gather.15.cloned.1.call-update) | async-done | bytes 10485776 | tf_op jit(solution)/shard_map/all_gather | solution.py:9
  455.6 9.6 %copy.11 = f32[16,8,32,640]{3,2,1,0:T(8,128)} copy(f32[16,8,32,640]{3,1,2,0:T(8,128)} %bitcast.39) | data formatting | bytes 20971520
  465.2 11.4 %bitcast_reduce_fusion = (f32[640,128]{0,1:T(8,128)}, f32[640,128]{0,1:T(8,128)}) fusion(f32[16,8,32,640]{3,2,1,0:T(8,128)} %copy.11, f32[16,8,32,640]{3,2,1,0:T(8,128)} %copy.10), kind=kLoop, calls=%fused_computation | loop fusion | flops 5079040 | bytes 21626880 | tf_op jit(solution)/shard_map/reduce_sum | solution.py:9
  476.6 139.4 %all-reduce.3.cloned.1.call-done = f32[1280,128]{0,1:T(8,128)} async-done(((f32[1280,128]{0,1:T(8,128)}), f32[1280,128]{0,1:T(8,128)}) %all-reduce.3.cloned.1.call-update) | async-done | bytes 655376 | tf_op jit(solution)/shard_map/psum | solution.py:53
  616.0 1.3 maximum_add_fusion
  617.4 0.0 copy-done.5
  617.4 0.5 fusion.5
  617.8 0.5 convolution_subtract_fusion.1
  618.3 0.0 copy-done.4
  618.3 0.5 fusion.13
  618.8 0.9 pad_maximum_fusion
  619.7 2.2 copy.7
  (3 shorter events, 0.0 us)
Async XLA Ops:
  6.5 7.9 %copy-start = (f32[1280,640]{1,0:T(8,128)S(1)}, f32[1280,640]{1,0:T(8,128)}, u32[]{:S(2)}) copy-start(f32[1280,640]{1,0:T(8,128)} %param.9) | copy-start | bytes 9830404
  6.5 126.3 %all-reduce.5.cloned.1.call-start = ((), (), s32[]{:S(2)}) async-start(), calls=%async_computation.1 | async-start | bytes 655360 | tf_op jit(solution)/shard_map/psum | solution.py:46
  9.6 4.1 copy-start.2
  13.7 0.7 copy-start.3
  17.3 161.7 %all-gather.9.cloned.1.call-start = ((), (), s32[]{:S(2)}) async-start(), calls=%async_computation.2 | async-start | bytes 2785280 | tf_op jit(solution)/shard_map/all_gather | solution.py:9
  19.0 204.3 %all-gather.11.cloned.1.call-start = ((), (), s32[]{:S(2)}) async-start(), calls=%async_computation.3 | async-start | bytes 2785280 | tf_op jit(solution)/shard_map/all_gather | solution.py:9
  20.7 319.5 %all-gather.13.cloned.1.call-start = ((), (), s32[]{:S(2)}) async-start(), calls=%async_computation.4 | async-start | bytes 10813440 | tf_op jit(solution)/shard_map/all_gather | solution.py:9
  134.7 320.9 %all-gather.15.cloned.1.call-start = ((), (), s32[]{:S(2)}) async-start(), calls=%async_computation.5 | async-start | bytes 10813440 | tf_op jit(solution)/shard_map/all_gather | solution.py:9
  135.3 480.7 %all-reduce.3.cloned.1.call-start = ((), (), s32[]{:S(2)}) async-start(), calls=%async_computation | async-start | bytes 1310720 | tf_op jit(solution)/shard_map/psum | solution.py:53
  223.3 2.5 copy-start.1
  465.2 152.1 %copy-start.5 = (f32[64,64]{1,0:T(8,128)S(1)}, f32[64,64]{1,0:T(8,128)}, u32[]{:S(2)}) copy-start(f32[64,64]{1,0:T(8,128)} %param.8) | copy-start | bytes 49156
  476.6 141.7 %copy-start.4 = (f32[64,64]{1,0:T(8,128)S(1)}, f32[64,64]{1,0:T(8,128)}, u32[]{:S(2)}) copy-start(f32[64,64]{1,0:T(8,128)} %param.7) | copy-start | bytes 49156
Sparse Core Ops, SparseCore 0:
  17.4 115.3 all-reduce.4
  135.2 43.7 all-gather.8
  181.3 41.8 all-gather.10
  226.9 113.1 all-gather.12
  343.8 111.7 all-gather.14
  459.2 156.7 all-reduce.2
